TPU v7x, 32 devices: a whole 2x2x4 slice. The times are simulated.
32 devices in a mesh: gx: 4 (over y, core), gy: 4 (over z), gz: 2 (over x).
Axes of the slice: x: 2, y: 2, z: 4, core: 2. Of those that a mesh axis runs over, the one named last changes fastest.
Arguments:
- right_side: bfloat16 [16384, 1024], P(('gx', 'gy', 'gz')), may hold values from -6 to 6
- projector: bfloat16 [16384, 256], P(('gx', 'gy', 'gz')), may hold values from -0.25 to 0.25
- translations: bfloat16 [32, 5, 256, 512], P(('gx', 'gy', 'gz')), may hold values from -0.25 to 0.25
- evaluator: bfloat16 [16384, 256], P(('gx', 'gy', 'gz')), may hold values from -0.375 to 0.375
Outputs:
- product: bfloat16 [16384, 1024], P(('gx', 'gy', 'gz'))
All inputs are finite; a program needn't handle non-finite values.
Results may differ from a plain program's by a relative error of at most 0.02.
Values may be sent and summed in bfloat16 or wider, within the bound.
A program may use at most 64 MiB of HBM per device.

v0:
```python
import jax
import jax.numpy as jnp
from jax import lax
from jax.sharding import PartitionSpec as P


def from_partner(block, axis, stride):
    count = lax.axis_size(axis)
    route = []
    for low in range(count):
        high = low | 1 << stride
        if high != low and high < count:
            route += [(low, high), (high, low)]
    return lax.ppermute(block, axis, route)


def translate(mapping, own_part, partner):
    rank_size = mapping.shape[0]
    total = jnp.dot(mapping[:, :rank_size], own_part, preferred_element_type=jnp.float32)
    total = total + jnp.dot(mapping[:, rank_size:], partner, preferred_element_type=jnp.float32)
    return total.astype(jnp.bfloat16)


def butterfly(column_parts, translation, swap_high, swap_middle, swap_low):
    height = 0
    plan = [
        (swap_high, lax.axis_size("gx").bit_length() - 1),
        (swap_middle, lax.axis_size("gy").bit_length() - 1),
        (swap_low, lax.axis_size("gz").bit_length() - 1),
    ]
    for mover, count in plan:
        for which_bit in range(count):
            partners = [mover(column, which_bit) for column in column_parts]
            column_parts = [
                translate(translation[height], column, partner)
                for column, partner in zip(column_parts, partners)
            ]
            height += 1
    return column_parts


def body(right_side, projector, translations, evaluator):
    translation = translations[0]
    coefficients = jnp.dot(projector.T, right_side, preferred_element_type=jnp.float32).astype(
        jnp.bfloat16
    )
    middle = coefficients.shape[1] // 2
    column_parts = [coefficients[:, :middle], coefficients[:, middle:]]
    column_parts = butterfly(
        column_parts,
        translation,
        lambda column, which_bit: from_partner(column, "gx", which_bit),
        lambda column, which_bit: from_partner(column, "gy", which_bit),
        lambda column, which_bit: from_partner(column, "gz", which_bit),
    )
    coefficients = jnp.concatenate(column_parts, axis=1)
    return jnp.dot(evaluator, coefficients, preferred_element_type=jnp.float32).astype(jnp.bfloat16)


def solution(mesh):
    placed = (
        P(("gx", "gy", "gz"), None),
        P(("gx", "gy", "gz"), None),
        P(("gx", "gy", "gz"), None, None, None),
        P(("gx", "gy", "gz"), None),
    )
    return jax.shard_map(
        body, mesh=mesh, in_specs=placed, out_specs=P(("gx", "gy", "gz"), None), check_vma=False
    )
```

profile of v0, /device:TPU:0, one launch (start us, length us, event | category | flops | bytes accessed | tf_op | source)
XLA Modules:
  0.0 58.1 jit_solution(2608465166673631507)
XLA Ops:
  0.0 1.2 %copy-done = bf16[512,1024]{1,0:T(8,128)(2,1)S(1)} copy-done((bf16[512,1024]{1,0:T(8,128)(2,1)S(1)}, bf16[512,1024]{1,0:T(8,128)(2,1)}, u32[]{:S(2)}) %copy-start) | copy-done | bytes 1048600
  1.2 1.4 %convolution_convert_fusion.1 = bf16[256,1024]{1,0:T(8,128)(2,1)S(1)} fusion(bf16[512,256]{1,0:T(8,128)(2,1)} %param.5, bf16[512,1024]{1,0:T(8,128)(2,1)S(1)} %copy-done), kind=kOutput, calls=%fused_computation.2 | convolution fusion | flops 268697600 | bytes 1835008 | tf_op jit(solution)/shard_map/dot_general | solution.py:44
  2.7 0.6 collective-permute-start
  3.5 0.3 fusion.42
  3.7 0.3 fusion.44
  4.0 0.4 collective-permute-done
  4.4 0.3 fusion.1
  4.7 2.9 %collective-permute-start.1 = (bf16[256,512]{0,1:T(8,128)(2,1)S(1)}, bf16[256,512]{0,1:T(8,128)(2,1)S(1)}, u32[]{:S(2)}, u32[]{:S(2)}) collective-permute-start(bf16[256,512]{0,1:T(8,128)(2,1)S(1)} %bitcast.46), channel_id=1, source_target_pairs={{0,16},{16,0},{8,24},{24,8},{1,17},{17,1},{9,25},{25,9},{2,18},{18... | collective-permute-start | bytes 786440 | tf_op jit(solution)/shard_map/ppermute | solution.py:14
  7.6 0.3 fusion.6
  8.5 6.3 %collective-permute-done.1 = bf16[256,512]{0,1:T(8,128)(2,1)S(1)} collective-permute-done((bf16[256,512]{0,1:T(8,128)(2,1)S(1)}, bf16[256,512]{0,1:T(8,128)(2,1)S(1)}, u32[]{:S(2)}, u32[]{:S(2)}) %collective-permute-start.1) | collective-permute-done | bytes 262176 | tf_op jit(solution)/shard_map/ppermute | solution.py:14
  15.0 2.1 %collective-permute-start.2 = (bf16[256,512]{0,1:T(8,128)(2,1)S(1)}, bf16[256,512]{0,1:T(8,128)(2,1)S(1)}, u32[]{:S(2)}, u32[]{:S(2)}) collective-permute-start(bf16[256,512]{0,1:T(8,128)(2,1)S(1)} %bitcast.48), channel_id=1, source_target_pairs={{0,2},{2,0},{4,6},{6,4},{1,3},{3,1},{5,7},{7,5},{8,10},{10,8},{12,... | collective-permute-start | bytes 786440 | tf_op jit(solution)/shard_map/ppermute | solution.py:14
  17.2 2.7 %collective-permute-done.6 = bf16[256,512]{0,1:T(8,128)(2,1)S(1)} collective-permute-done((bf16[256,512]{0,1:T(8,128)(2,1)S(1)}, bf16[256,512]{0,1:T(8,128)(2,1)S(1)}, u32[]{:S(2)}, u32[]{:S(2)}) %collective-permute-start.6) | collective-permute-done | bytes 262176 | tf_op jit(solution)/shard_map/ppermute | solution.py:14
  20.4 1.9 %collective-permute-start.7 = (bf16[256,512]{0,1:T(8,128)(2,1)S(1)}, bf16[256,512]{0,1:T(8,128)(2,1)S(1)}, u32[]{:S(2)}, u32[]{:S(2)}) collective-permute-start(bf16[256,512]{0,1:T(8,128)(2,1)S(1)} %bitcast.49), channel_id=1, source_target_pairs={{0,2},{2,0},{4,6},{6,4},{1,3},{3,1},{5,7},{7,5},{8,10},{10,8},{12,... | collective-permute-start | bytes 786440 | tf_op jit(solution)/shard_map/ppermute | solution.py:14
  22.5 0.3 fusion.3
  22.8 2.6 %collective-permute-start.3 = (bf16[256,512]{0,1:T(8,128)(2,1)S(1)}, bf16[256,512]{0,1:T(8,128)(2,1)S(1)}, u32[]{:S(2)}, u32[]{:S(2)}) collective-permute-start(bf16[256,512]{0,1:T(8,128)(2,1)S(1)} %bitcast.50), channel_id=1, source_target_pairs={{0,4},{4,0},{2,6},{6,2},{1,5},{5,1},{3,7},{7,3},{8,12},{12,8},{10,... | collective-permute-start | bytes 786440 | tf_op jit(solution)/shard_map/ppermute | solution.py:14
  25.4 7.7 %collective-permute-done.7 = bf16[256,512]{0,1:T(8,128)(2,1)S(1)} collective-permute-done((bf16[256,512]{0,1:T(8,128)(2,1)S(1)}, bf16[256,512]{0,1:T(8,128)(2,1)S(1)}, u32[]{:S(2)}, u32[]{:S(2)}) %collective-permute-start.7) | collective-permute-done | bytes 262176 | tf_op jit(solution)/shard_map/ppermute | solution.py:14
  33.6 0.6 collective-permute-start.8
  34.4 8.5 %collective-permute-done.3 = bf16[256,512]{0,1:T(8,128)(2,1)S(1)} collective-permute-done((bf16[256,512]{0,1:T(8,128)(2,1)S(1)}, bf16[256,512]{0,1:T(8,128)(2,1)S(1)}, u32[]{:S(2)}, u32[]{:S(2)}) %collective-permute-start.3) | collective-permute-done | bytes 262176 | tf_op jit(solution)/shard_map/ppermute | solution.py:14
  43.2 1.5 %collective-permute-start.4 = (bf16[256,512]{0,1:T(8,128)(2,1)S(1)}, bf16[256,512]{0,1:T(8,128)(2,1)S(1)}, u32[]{:S(2)}, u32[]{:S(2)}) collective-permute-start(bf16[256,512]{0,1:T(8,128)(2,1)S(1)} %bitcast.45), channel_id=1, source_target_pairs={{0,1},{1,0},{2,3},{3,2},{4,5},{5,4},{6,7},{7,6},{8,9},{9,8},{10,11... | collective-permute-start | bytes 786440 | tf_op jit(solution)/shard_map/ppermute | solution.py:14
  44.8 3.1 %collective-permute-done.8 = bf16[256,512]{0,1:T(8,128)(2,1)S(1)} collective-permute-done((bf16[256,512]{0,1:T(8,128)(2,1)S(1)}, bf16[256,512]{0,1:T(8,128)(2,1)S(1)}, u32[]{:S(2)}, u32[]{:S(2)}) %collective-permute-start.8) | collective-permute-done | bytes 262176 | tf_op jit(solution)/shard_map/ppermute | solution.py:14
  48.4 1.5 %collective-permute-start.9 = (bf16[256,512]{0,1:T(8,128)(2,1)S(1)}, bf16[256,512]{0,1:T(8,128)(2,1)S(1)}, u32[]{:S(2)}, u32[]{:S(2)}) collective-permute-start(bf16[256,512]{0,1:T(8,128)(2,1)S(1)} %bitcast.52), channel_id=1, source_target_pairs={{0,1},{1,0},{2,3},{3,2},{4,5},{5,4},{6,7},{7,6},{8,9},{9,8},{10,11... | collective-permute-start | bytes 786440 | tf_op jit(solution)/shard_map/ppermute | solution.py:14
  50.5 5.6 %collective-permute-done.9 = bf16[256,512]{0,1:T(8,128)(2,1)S(1)} collective-permute-done((bf16[256,512]{0,1:T(8,128)(2,1)S(1)}, bf16[256,512]{0,1:T(8,128)(2,1)S(1)}, u32[]{:S(2)}, u32[]{:S(2)}) %collective-permute-start.9) | collective-permute-done | bytes 262176 | tf_op jit(solution)/shard_map/ppermute | solution.py:14
  56.3 0.5 fusion
  56.8 1.3 %copy.5 = bf16[512,1024]{1,0:T(8,128)(2,1)} copy(bf16[512,1024]{0,1:T(8,128)(2,1)S(1)} %fusion) | data formatting | bytes 2097152 | tf_op jit(solution)/shard_map/convert_element_type | solution.py:57
  (27 shorter events, 4.2 us)
Async XLA Ops:
  0.0 1.2 %copy-start = (bf16[512,1024]{1,0:T(8,128)(2,1)S(1)}, bf16[512,1024]{1,0:T(8,128)(2,1)}, u32[]{:S(2)}) copy-start(bf16[512,1024]{1,0:T(8,128)(2,1)} %param.4) | copy-start | bytes 3145732
  0.0 3.3 %copy-start.1 = (bf16[1,5,256,512]{3,2,1,0:T(8,128)(2,1)S(1)}, bf16[1,5,256,512]{3,2,1,0:T(8,128)(2,1)}, u32[]{:S(2)}) copy-start(bf16[1,5,256,512]{3,2,1,0:T(8,128)(2,1)} %param.6) | copy-start | bytes 3932164
  2.7 1.7 %collective-permute-start = (bf16[256,512]{1,0:T(8,128)(2,1)S(1)}, bf16[256,512]{1,0:T(8,128)(2,1)S(1)}, u32[]{:S(2)}, u32[]{:S(2)}) collective-permute-start(bf16[256,512]{1,0:T(8,128)(2,1)S(1)} %get-tuple-element.10), channel_id=1, source_target_pairs={{0,8},{8,0},{16,24},{24,16},{1,9},{9,1},{17,25},{25,17},{2,10},{10... | collective-permute-start | bytes 786440 | tf_op jit(solution)/shard_map/ppermute | solution.py:14
  3.2 4.4 %collective-permute-start.5 = (bf16[256,512]{1,0:T(8,128)(2,1)S(1)}, bf16[256,512]{1,0:T(8,128)(2,1)S(1)}, u32[]{:S(2)}, u32[]{:S(2)}) collective-permute-start(bf16[256,512]{1,0:T(8,128)(2,1)S(1)} %get-tuple-element.11), channel_id=1, source_target_pairs={{0,8},{8,0},{16,24},{24,16},{1,9},{9,1},{17,25},{25,17},{2,10},{10... | collective-permute-start | bytes 786440 | tf_op jit(solution)/shard_map/ppermute | solution.py:14
  4.7 10.1 %collective-permute-start.1 = (bf16[256,512]{0,1:T(8,128)(2,1)S(1)}, bf16[256,512]{0,1:T(8,128)(2,1)S(1)}, u32[]{:S(2)}, u32[]{:S(2)}) collective-permute-start(bf16[256,512]{0,1:T(8,128)(2,1)S(1)} %bitcast.46), channel_id=1, source_target_pairs={{0,16},{16,0},{8,24},{24,8},{1,17},{17,1},{9,25},{25,9},{2,18},{18... | collective-permute-start | bytes 786440 | tf_op jit(solution)/shard_map/ppermute | solution.py:14
  7.9 12.0 %collective-permute-start.6 = (bf16[256,512]{0,1:T(8,128)(2,1)S(1)}, bf16[256,512]{0,1:T(8,128)(2,1)S(1)}, u32[]{:S(2)}, u32[]{:S(2)}) collective-permute-start(bf16[256,512]{0,1:T(8,128)(2,1)S(1)} %bitcast.47), channel_id=1, source_target_pairs={{0,16},{16,0},{8,24},{24,8},{1,17},{17,1},{9,25},{25,9},{2,18},{18... | collective-permute-start | bytes 786440 | tf_op jit(solution)/shard_map/ppermute | solution.py:14
  15.0 7.5 %collective-permute-start.2 = (bf16[256,512]{0,1:T(8,128)(2,1)S(1)}, bf16[256,512]{0,1:T(8,128)(2,1)S(1)}, u32[]{:S(2)}, u32[]{:S(2)}) collective-permute-start(bf16[256,512]{0,1:T(8,128)(2,1)S(1)} %bitcast.48), channel_id=1, source_target_pairs={{0,2},{2,0},{4,6},{6,4},{1,3},{3,1},{5,7},{7,5},{8,10},{10,8},{12,... | collective-permute-start | bytes 786440 | tf_op jit(solution)/shard_map/ppermute | solution.py:14
  20.4 12.7 %collective-permute-start.7 = (bf16[256,512]{0,1:T(8,128)(2,1)S(1)}, bf16[256,512]{0,1:T(8,128)(2,1)S(1)}, u32[]{:S(2)}, u32[]{:S(2)}) collective-permute-start(bf16[256,512]{0,1:T(8,128)(2,1)S(1)} %bitcast.49), channel_id=1, source_target_pairs={{0,2},{2,0},{4,6},{6,4},{1,3},{3,1},{5,7},{7,5},{8,10},{10,8},{12,... | collective-permute-start | bytes 786440 | tf_op jit(solution)/shard_map/ppermute | solution.py:14
  22.8 20.2 %collective-permute-start.3 = (bf16[256,512]{0,1:T(8,128)(2,1)S(1)}, bf16[256,512]{0,1:T(8,128)(2,1)S(1)}, u32[]{:S(2)}, u32[]{:S(2)}) collective-permute-start(bf16[256,512]{0,1:T(8,128)(2,1)S(1)} %bitcast.50), channel_id=1, source_target_pairs={{0,4},{4,0},{2,6},{6,2},{1,5},{5,1},{3,7},{7,3},{8,12},{12,8},{10,... | collective-permute-start | bytes 786440 | tf_op jit(solution)/shard_map/ppermute | solution.py:14
  33.6 14.2 %collective-permute-start.8 = (bf16[256,512]{0,1:T(8,128)(2,1)S(1)}, bf16[256,512]{0,1:T(8,128)(2,1)S(1)}, u32[]{:S(2)}, u32[]{:S(2)}) collective-permute-start(bf16[256,512]{0,1:T(8,128)(2,1)S(1)} %bitcast.51), channel_id=1, source_target_pairs={{0,4},{4,0},{2,6},{6,2},{1,5},{5,1},{3,7},{7,3},{8,12},{12,8},{10,... | collective-permute-start | bytes 786440 | tf_op jit(solution)/shard_map/ppermute | solution.py:14
  43.2 7.0 %collective-permute-start.4 = (bf16[256,512]{0,1:T(8,128)(2,1)S(1)}, bf16[256,512]{0,1:T(8,128)(2,1)S(1)}, u32[]{:S(2)}, u32[]{:S(2)}) collective-permute-start(bf16[256,512]{0,1:T(8,128)(2,1)S(1)} %bitcast.45), channel_id=1, source_target_pairs={{0,1},{1,0},{2,3},{3,2},{4,5},{5,4},{6,7},{7,6},{8,9},{9,8},{10,11... | collective-permute-start | bytes 786440 | tf_op jit(solution)/shard_map/ppermute | solution.py:14
  48.4 7.7 %collective-permute-start.9 = (bf16[256,512]{0,1:T(8,128)(2,1)S(1)}, bf16[256,512]{0,1:T(8,128)(2,1)S(1)}, u32[]{:S(2)}, u32[]{:S(2)}) collective-permute-start(bf16[256,512]{0,1:T(8,128)(2,1)S(1)} %bitcast.52), channel_id=1, source_target_pairs={{0,1},{1,0},{2,3},{3,2},{4,5},{5,4},{6,7},{7,6},{8,9},{9,8},{10,11... | collective-permute-start | bytes 786440 | tf_op jit(solution)/shard_map/ppermute | solution.py:14
  50.2 6.1 %copy-start.2 = (bf16[512,256]{1,0:T(8,128)(2,1)S(1)}, bf16[512,256]{1,0:T(8,128)(2,1)}, u32[]{:S(2)}) copy-start(bf16[512,256]{1,0:T(8,128)(2,1)} %param.7) | copy-start | bytes 786436
where the time goes:
time: 58.3 us; the launch traced here: 58.1 us
  waiting for transfers between devices  34.2 us (59%)
  starting transfers between devices  14 us (24%)
  matrix products  7.05 us (12%)
  local copies, waits for them, and re-layouts  2.71 us (5%)
    ppermute x10, waiting for transfers between devices, from_partner(): return lax.ppermute(block, axis, route)  34.2 us
    ppermute x10, starting transfers between devices, from_partner(): return lax.ppermute(block, axis, route)  14 us
    dot_general x10, matrix products, translate(): jnp.dot(mapping[:, rank_size:], partner, preferred_element_type=jnp.float32)  2.63 us
    dot_general x10, matrix products, translate(): jnp.dot(mapping[:, :rank_size], own_part, preferred_element_type=jnp.floa...  2.56 us
    dot_general x1, matrix products, body(): jnp.dot(projector.T, right_side, preferred_element_type=jnp.float32)  1.4 us
    convert_element_type x1, local copies, waits for them, and re-layouts, body(): jnp.dot(evaluator, coefficients, preferred_element_type=jnp.float32)  1.32 us
    unnamed x6, local copies, waits for them, and re-layouts  1.23 us
  transfers between devices with their start and end apart: 10, of which 7 were waited for; matrix products, arithmetic and copies ran while one was open for 9% of the time, Pallas kernels for 0%

commit v1 on v0

v1 whole, which is shorter than its diff:
```python
import functools

import jax
import jax.numpy as jnp
from jax import lax
from jax.experimental import pallas as pl
from jax.experimental.pallas import tpu as pltpu
from jax.sharding import PartitionSpec as P

MESH = pl.DeviceIdType.MESH
PIECE = 128


def level_plan(sizes):
    return [(axis, bit) for axis, size in sizes for bit in range(size.bit_length() - 1)]


def step_order(pieces, levels):
    offset = [0.0, 0.3] + [0.3 + 1.2 * k for k in range(1, levels)]
    steps = [(p + offset[l], -l, p, l) for p in range(pieces) for l in range(levels + 1)]
    return [(p, l) for _, _, p, l in sorted(steps)]


def kernel(plan, steps, right_hbm, projector_hbm, translation_hbm, out_ref,
           right, projector, projector_t, mapping, stack,
           right_sem, projector_sem, mapping_sem, send_sem, recv_sem):
    rank = out_ref.shape[0]
    pieces = out_ref.shape[1] // PIECE
    levels = len(plan)

    def columns(p):
        return pl.ds(p * PIECE, PIECE)

    loads = [pltpu.make_async_copy(projector_hbm, projector, projector_sem)]
    right_loads = [
        pltpu.make_async_copy(right_hbm.at[:, columns(p)], right.at[p], right_sem.at[p])
        for p in range(pieces)
    ]
    mapping_loads = [
        pltpu.make_async_copy(translation_hbm.at[l], mapping.at[l], mapping_sem.at[l])
        for l in range(levels)
    ]
    loads[0].start()
    right_loads[0].start()
    for copy in mapping_loads[:2] + right_loads[1:] + mapping_loads[2:]:
        copy.start()

    partners = []
    for axis, bit in plan:
        me = lax.axis_index(axis)
        step = 1 << bit
        partners.append({axis: me + step - 2 * step * ((me // step) % 2)})
    barrier = pltpu.get_barrier_semaphore()
    for partner in partners:
        pl.semaphore_signal(barrier, inc=1, device_id=partner, device_id_type=MESH)

    def exchange(p, l):
        return pltpu.make_async_remote_copy(
            src_ref=stack.at[l, p, pl.ds(0, rank)],
            dst_ref=stack.at[l, p, pl.ds(rank, rank)],
            send_sem=send_sem.at[l, p],
            recv_sem=recv_sem.at[l, p],
            device_id=partners[l],
            device_id_type=MESH,
        )

    loads[0].wait()
    projector_t[...] = projector[...].T
    first = True
    mapped = set()
    for p, l in steps:
        if l == 0:
            right_loads[p].wait()
            value = jnp.dot(projector_t[...], right[p], preferred_element_type=jnp.float32)
        else:
            if l not in mapped:
                mapping_loads[l - 1].wait()
                mapped.add(l)
            exchange(p, l - 1).wait_recv()
            value = jnp.dot(mapping[l - 1], stack[l - 1, p], preferred_element_type=jnp.float32)
        value = value.astype(jnp.bfloat16)
        if l < levels:
            stack[l, p, pl.ds(0, rank)] = value
            if first:
                pl.semaphore_wait(barrier, levels)
                first = False
            exchange(p, l).start()
        else:
            out_ref[:, columns(p)] = value
    for l in range(levels):
        for p in range(pieces):
            exchange(p, l).wait_send()


def body(sizes, right_side, projector, translations, evaluator):
    plan = level_plan(sizes)
    levels = len(plan)
    leaf, width = right_side.shape
    rank = projector.shape[1]
    pieces = width // PIECE
    half = jnp.bfloat16
    any_space = pl.BlockSpec(memory_space=pl.ANY)
    coefficients = pl.pallas_call(
        functools.partial(kernel, plan, step_order(pieces, levels)),
        out_shape=jax.ShapeDtypeStruct((rank, width), half),
        in_specs=[any_space] * 3,
        out_specs=pl.BlockSpec(memory_space=pltpu.VMEM),
        scratch_shapes=[
            pltpu.VMEM((pieces, leaf, PIECE), half),
            pltpu.VMEM((leaf, rank), half),
            pltpu.VMEM((rank, leaf), half),
            pltpu.VMEM((levels, rank, 2 * rank), half),
            pltpu.VMEM((levels, pieces, 2 * rank, PIECE), half),
            pltpu.SemaphoreType.DMA((pieces,)),
            pltpu.SemaphoreType.DMA,
            pltpu.SemaphoreType.DMA((levels,)),
            pltpu.SemaphoreType.DMA((levels, pieces)),
            pltpu.SemaphoreType.DMA((levels, pieces)),
        ],
        compiler_params=pltpu.CompilerParams(collective_id=0, has_side_effects=True),
    )(right_side, projector, translations[0])
    return jnp.dot(evaluator, coefficients, preferred_element_type=jnp.float32).astype(half)


def solution(mesh):
    placed = (
        P(("gx", "gy", "gz"), None),
        P(("gx", "gy", "gz"), None),
        P(("gx", "gy", "gz"), None, None, None),
        P(("gx", "gy", "gz"), None),
    )
    sizes = [(axis, mesh.shape[axis]) for axis in ("gx", "gy", "gz")]
    return jax.shard_map(
        functools.partial(body, sizes), mesh=mesh, in_specs=placed,
        out_specs=P(("gx", "gy", "gz"), None), check_vma=False,
    )
```

time: 58.3 us -> 50.2 us (0.86)
  Pallas kernels: 0 us -> 47.2 us
  waiting for transfers between devices: 34.2 us -> 0 us
  starting transfers between devices: 14 us -> 0 us
  matrix products: 7.05 us -> 1.53 us
  local copies, waits for them, and re-layouts: 2.71 us -> 1.32 us
    pallas_call x0 -> x1, Pallas kernels: none -> 47.2 us  [body(): pl.pallas_call(functools.partial(kernel, plan, step_order(pieces, levels)...]
    ppermute x10 -> x0, waiting for transfers between devices: 34.2 us -> none  [from_partner(): return lax.ppermute(block, axis, route)]
    ppermute x10 -> x0, starting transfers between devices: 14 us -> none  [from_partner(): return lax.ppermute(block, axis, route)]
    dot_general x21 -> x0, matrix products: 6.59 us -> none  [the longest x10 2.63 us: translate(): jnp.dot(mapping[:, rank_size:], partner, preferred_element_type=jnp.float32)]
    unnamed x6 -> x2, local copies, waits for them, and re-layouts: 1.23 us -> 0.01 us
    dot_general x1, matrix products: 0.46 us -> 1.53 us  [body(): jnp.dot(evaluator, coefficients, preferred_element_type=jnp.float32)]
  transfers between devices with their start and end apart: 10 -> 0, of which waited for: 7 -> 0; matrix products, arithmetic and copies ran while one was open for 9% -> 0% of each run, Pallas kernels for 0% -> 0%
where the time goes in v1:
time: 50.2 us; the launch traced here: 50 us
  Pallas kernels  47.2 us (94%)
  matrix products  1.53 us (3%)
  local copies, waits for them, and re-layouts  1.32 us (3%)
    pallas_call x1, Pallas kernels, body(): pl.pallas_call(functools.partial(kernel, plan, step_order(pieces, levels)...  47.2 us
    dot_general x1, matrix products, body(): jnp.dot(evaluator, coefficients, preferred_element_type=jnp.float32)  1.53 us
    convert_element_type x1, local copies, waits for them, and re-layouts, body(): jnp.dot(evaluator, coefficients, preferred_element_type=jnp.float32)  1.32 us

profile of v1, /device:TPU:0, one launch (start us, length us, event | category | flops | bytes accessed | tf_op | source)
XLA Modules:
  0.0 50.0 jit_solution(5444655644410389030)
XLA Ops:
  0.0 0.0 copy-start
  0.0 47.2 %shard_map.46 = bf16[256,1024]{1,0:T(8,128)(2,1)} custom-call(bf16[512,1024]{1,0:T(8,128)(2,1)} %right_hbm.1, bf16[512,256]{1,0:T(8,128)(2,1)} %projector_hbm.1, bf16[5,256,512]{2,1,0:T(8,128)(2,1)} %bitcast.5), custom_call_target="tpu_custom_call" | custom-call | tf_op jit(solution)/shard_map/pallas_call | solution.py:103
  47.2 0.0 copy-done
  47.2 1.5 %fusion = bf16[512,1024]{0,1:T(8,128)(2,1)S(1)} fusion(bf16[256,1024]{1,0:T(8,128)(2,1)} %shard_map.46, bf16[512,256]{1,0:T(8,128)(2,1)S(1)} %copy-done), kind=kOutput, calls=%fused_computation.1 | convolution fusion | flops 268959744 | bytes 1835008 | tf_op jit(solution)/shard_map/dot_general | solution.py:122
  48.7 1.3 %copy.5 = bf16[512,1024]{1,0:T(8,128)(2,1)} copy(bf16[512,1024]{0,1:T(8,128)(2,1)S(1)} %fusion) | data formatting | bytes 2097152 | tf_op jit(solution)/shard_map/convert_element_type | solution.py:122
Async XLA Ops:
  0.0 47.2 %copy-start = (bf16[512,256]{1,0:T(8,128)(2,1)S(1)}, bf16[512,256]{1,0:T(8,128)(2,1)}, u32[]{:S(2)}) copy-start(bf16[512,256]{1,0:T(8,128)(2,1)} %param.7) | copy-start | bytes 786436

commit v2 on v1

v2 whole, which is shorter than its diff:
```python
import functools

import jax
import jax.numpy as jnp
from jax import lax
from jax.experimental import pallas as pl
from jax.experimental.pallas import tpu as pltpu
from jax.sharding import PartitionSpec as P

MESH = pl.DeviceIdType.MESH
PIECE = 128


def level_plan(sizes):
    return [(axis, bit) for axis, size in sizes for bit in range(size.bit_length() - 1)]


def step_order(plan, pieces):
    steps = []
    when = 0.0
    for l in range(len(plan) + 1):
        steps += [(p + when, p, l, False) for p in range(pieces)]
        if l < len(plan):
            if relayed(plan[l]):
                when += 1.1
                steps += [(p + when, p, l, True) for p in range(pieces)]
            when += 0.4 if l == 0 else 1.0
    steps.sort(key=lambda step: (step[0], -step[2]))
    return [step[1:] for step in steps]


def relayed(level):
    return level == ("gy", 1)


def kernel(plan, steps, right_hbm, projector_hbm, translation_hbm, out_ref,
           right, projector, projector_t, mapping, stack, relay,
           right_sem, projector_sem, mapping_sem, send_sem, recv_sem,
           relay_send, relay_recv):
    rank = out_ref.shape[0]
    pieces = out_ref.shape[1] // PIECE
    levels = len(plan)
    has_relay = any(relayed(level) for level in plan)

    def columns(p):
        return pl.ds(p * PIECE, PIECE)

    projector_load = pltpu.make_async_copy(projector_hbm, projector, projector_sem)
    right_loads = [
        pltpu.make_async_copy(right_hbm.at[:, columns(p)], right.at[p], right_sem.at[p])
        for p in range(pieces)
    ]
    mapping_loads = [
        pltpu.make_async_copy(translation_hbm.at[l], mapping.at[l], mapping_sem.at[l])
        for l in range(levels)
    ]
    projector_load.start()
    right_loads[0].start()
    for copy in mapping_loads[:2] + right_loads[1:] + mapping_loads[2:]:
        copy.start()

    place = lax.axis_index("gy")
    side = (place // 2) % 2
    towards = place + 1 - 2 * side
    middle = (place % 2 + side) % 2

    partners = []
    for axis, bit in plan:
        me = lax.axis_index(axis)
        step = 1 << bit
        partners.append({axis: me + step - 2 * step * ((me // step) % 2)})
    barrier = pltpu.get_barrier_semaphore()
    direct = [partner for partner, level in zip(partners, plan) if not relayed(level)]
    for partner in direct:
        pl.semaphore_signal(barrier, inc=1, device_id=partner, device_id_type=MESH)
    if has_relay:
        @pl.when(middle == 1)
        def _():
            pl.semaphore_signal(
                barrier, inc=1, device_id={"gy": towards}, device_id_type=MESH
            )

    def exchange(p, l):
        if relayed(plan[l]):
            return pltpu.make_async_remote_copy(
                src_ref=stack.at[l, p, pl.ds(0, rank)],
                dst_ref=relay.at[side, p],
                send_sem=send_sem.at[l, p],
                recv_sem=relay_recv.at[side, p],
                device_id={"gy": towards},
                device_id_type=MESH,
            )
        return pltpu.make_async_remote_copy(
            src_ref=stack.at[l, p, pl.ds(0, rank)],
            dst_ref=stack.at[l, p, pl.ds(rank, rank)],
            send_sem=send_sem.at[l, p],
            recv_sem=recv_sem.at[l, p],
            device_id=partners[l],
            device_id_type=MESH,
        )

    def forward(p, l, down):
        return pltpu.make_async_remote_copy(
            src_ref=relay.at[down, p],
            dst_ref=stack.at[l, p, pl.ds(rank, rank)],
            send_sem=relay_send.at[down, p],
            recv_sem=recv_sem.at[l, p],
            device_id={"gy": place + 1 - 2 * down},
            device_id_type=MESH,
        )

    def arrived(p, down):
        return pltpu.make_async_copy(relay.at[down, p], relay.at[down, p], relay_recv.at[down, p])

    def landed(p, l):
        half = stack.at[l, p, pl.ds(rank, rank)]
        return pltpu.make_async_copy(half, half, recv_sem.at[l, p])

    projector_load.wait()
    projector_t[...] = projector[...].T
    first = True
    mapped = set()
    for p, l, is_relay in steps:
        if is_relay:
            @pl.when(middle == 1)
            def _():
                for down in range(2):
                    arrived(p, down).wait()
                    forward(p, l, down).start()
            continue
        if l == 0:
            right_loads[p].wait()
            value = jnp.dot(projector_t[...], right[p], preferred_element_type=jnp.float32)
        else:
            if l not in mapped:
                mapping_loads[l - 1].wait()
                mapped.add(l)
            landed(p, l - 1).wait()
            value = jnp.dot(mapping[l - 1], stack[l - 1, p], preferred_element_type=jnp.float32)
        value = value.astype(jnp.bfloat16)
        if l < levels:
            stack[l, p, pl.ds(0, rank)] = value
            if first:
                pl.semaphore_wait(barrier, len(direct) + (middle if has_relay else 0))
                first = False
            exchange(p, l).start()
        else:
            out_ref[:, columns(p)] = value
    for l in range(levels):
        for p in range(pieces):
            exchange(p, l).wait_send()
    if has_relay:
        @pl.when(middle == 1)
        def _():
            for l in range(levels):
                if relayed(plan[l]):
                    for p in range(pieces):
                        for down in range(2):
                            forward(p, l, down).wait_send()


def evaluate_kernel(evaluator, coefficients, out):
    out[...] = jnp.dot(
        evaluator[...], coefficients[...], preferred_element_type=jnp.float32
    ).astype(out.dtype)


def body(sizes, right_side, projector, translations, evaluator):
    plan = level_plan(sizes)
    levels = len(plan)
    leaf, width = right_side.shape
    rank = projector.shape[1]
    pieces = width // PIECE
    half = jnp.bfloat16
    any_space = pl.BlockSpec(memory_space=pl.ANY)
    coefficients = pl.pallas_call(
        functools.partial(kernel, plan, step_order(plan, pieces)),
        out_shape=jax.ShapeDtypeStruct((rank, width), half),
        in_specs=[any_space] * 3,
        out_specs=pl.BlockSpec(memory_space=pltpu.VMEM),
        scratch_shapes=[
            pltpu.VMEM((pieces, leaf, PIECE), half),
            pltpu.VMEM((leaf, rank), half),
            pltpu.VMEM((rank, leaf), half),
            pltpu.VMEM((levels, rank, 2 * rank), half),
            pltpu.VMEM((levels, pieces, 2 * rank, PIECE), half),
            pltpu.VMEM((2, pieces, rank, PIECE), half),
            pltpu.SemaphoreType.DMA((pieces,)),
            pltpu.SemaphoreType.DMA,
            pltpu.SemaphoreType.DMA((levels,)),
            pltpu.SemaphoreType.DMA((levels, pieces)),
            pltpu.SemaphoreType.DMA((levels, pieces)),
            pltpu.SemaphoreType.DMA((2, pieces)),
            pltpu.SemaphoreType.DMA((2, pieces)),
        ],
        compiler_params=pltpu.CompilerParams(collective_id=0, has_side_effects=True),
    )(right_side, projector, translations[0])
    rows = leaf // 4
    return pl.pallas_call(
        evaluate_kernel,
        out_shape=jax.ShapeDtypeStruct((leaf, width), half),
        grid=(4,),
        in_specs=[
            pl.BlockSpec((rows, rank), lambda i: (i, 0)),
            pl.BlockSpec((rank, width), lambda i: (0, 0)),
        ],
        out_specs=pl.BlockSpec((rows, width), lambda i: (i, 0)),
    )(evaluator, coefficients)


def solution(mesh):
    placed = (
        P(("gx", "gy", "gz"), None),
        P(("gx", "gy", "gz"), None),
        P(("gx", "gy", "gz"), None, None, None),
        P(("gx", "gy", "gz"), None),
    )
    sizes = [(axis, mesh.shape[axis]) for axis in ("gx", "gy", "gz")]
    return jax.shard_map(
        functools.partial(body, sizes), mesh=mesh, in_specs=placed,
        out_specs=P(("gx", "gy", "gz"), None), check_vma=False,
    )
```

time: 50.2 us -> 62.4 us (1.24)
  Pallas kernels: 47.2 us -> 62.1 us
  matrix products: 1.53 us -> 0 us
  local copies, waits for them, and re-layouts: 1.32 us -> 0 us
    pallas_call x1 -> x2, Pallas kernels: 47.2 us -> 62.1 us  [the longest x1 58.3 us: body(): pl.pallas_call(functools.partial(kernel, plan, step_order(plan, pieces)),...]
    dot_general x1 -> x0, matrix products: 1.53 us -> none  [body(): jnp.dot(evaluator, coefficients, preferred_element_type=jnp.float32)]
    convert_element_type x1 -> x0, local copies, waits for them, and re-layouts: 1.32 us -> none  [body(): jnp.dot(evaluator, coefficients, preferred_element_type=jnp.float32)]
where the time goes in v2:
time: 62.4 us; the launch traced here: 62.1 us
  Pallas kernels  62.1 us (100%)
    pallas_call x1, Pallas kernels, body(): pl.pallas_call(functools.partial(kernel, plan, step_order(plan, pieces)),...  58.3 us
    pallas_call x1, Pallas kernels, body(): pl.pallas_call(evaluate_kernel, out_shape=jax.ShapeDtypeStruct((leaf, wid...  3.82 us

profile of v2, /device:TPU:0, one launch (start us, length us, event | category | flops | bytes accessed | tf_op | source)
XLA Modules:
  0.0 62.1 jit_solution(10332073808903828214)
XLA Ops:
  0.0 58.3 %shard_map.46.coefficients = bf16[256,1024]{1,0:T(8,128)(2,1)} custom-call(bf16[512,1024]{1,0:T(8,128)(2,1)} %right_hbm.1, bf16[512,256]{1,0:T(8,128)(2,1)} %projector_hbm.1, bf16[5,256,512]{2,1,0:T(8,128)(2,1)} %bitcast.1), custom_call_target="tpu_custom_call" | custom-call | tf_op jit(solution)/shard_map/pallas_call | solution.py:176
  58.3 3.8 %shard_map.47 = bf16[512,1024]{1,0:T(8,128)(2,1)} custom-call(bf16[512,256]{1,0:T(8,128)(2,1)} %evaluator.1, bf16[256,1024]{1,0:T(8,128)(2,1)} %shard_map.46.coefficients), custom_call_target="tpu_custom_call" | custom-call | tf_op jit(solution)/shard_map/pallas_call | solution.py:199

commit v3 on v1

--- a/solution.py
+++ b/solution.py
@@ -17,15 +17,16 @@
 
 def step_order(pieces, levels):
     offset = [0.0, 0.3] + [0.3 + 1.2 * k for k in range(1, levels)]
-    steps = [(p + offset[l], -l, p, l) for p in range(pieces) for l in range(levels + 1)]
+    steps = [(0.6 * p + offset[l], -l, p, l) for p in range(pieces) for l in range(levels + 1)]
     return [(p, l) for _, _, p, l in sorted(steps)]
 
 
-def kernel(plan, steps, right_hbm, projector_hbm, translation_hbm, out_ref,
-           right, projector, projector_t, mapping, stack,
-           right_sem, projector_sem, mapping_sem, send_sem, recv_sem):
-    rank = out_ref.shape[0]
-    pieces = out_ref.shape[1] // PIECE
+def kernel(plan, steps, right_hbm, projector_hbm, translation_hbm, evaluator_hbm, out_hbm,
+           right, projector, projector_t, mapping, stack, evaluator, out,
+           right_sem, projector_sem, mapping_sem, send_sem, recv_sem,
+           evaluator_sem, out_sem):
+    rank = projector.shape[1]
+    pieces = right.shape[0]
     levels = len(plan)
 
     def columns(p):
@@ -40,9 +41,10 @@
         pltpu.make_async_copy(translation_hbm.at[l], mapping.at[l], mapping_sem.at[l])
         for l in range(levels)
     ]
+    evaluator_load = pltpu.make_async_copy(evaluator_hbm, evaluator, evaluator_sem)
     loads[0].start()
     right_loads[0].start()
-    for copy in mapping_loads[:2] + right_loads[1:] + mapping_loads[2:]:
+    for copy in mapping_loads[:2] + right_loads[1:] + mapping_loads[2:] + [evaluator_load]:
         copy.start()
 
     partners = []
@@ -53,6 +55,9 @@
     barrier = pltpu.get_barrier_semaphore()
     for partner in partners:
         pl.semaphore_signal(barrier, inc=1, device_id=partner, device_id_type=MESH)
+
+    def store(p):
+        return pltpu.make_async_copy(out.at[p], out_hbm.at[:, columns(p)], out_sem.at[p])
 
     def exchange(p, l):
         return pltpu.make_async_remote_copy(
@@ -86,10 +91,16 @@
                 first = False
             exchange(p, l).start()
         else:
-            out_ref[:, columns(p)] = value
+            if p == 0:
+                evaluator_load.wait()
+            product = jnp.dot(evaluator[...], value, preferred_element_type=jnp.float32)
+            out[p] = product.astype(jnp.bfloat16)
+            store(p).start()
     for l in range(levels):
         for p in range(pieces):
             exchange(p, l).wait_send()
+    for p in range(pieces):
+        store(p).wait()
 
 
 def body(sizes, right_side, projector, translations, evaluator):
@@ -100,26 +111,29 @@
     pieces = width // PIECE
     half = jnp.bfloat16
     any_space = pl.BlockSpec(memory_space=pl.ANY)
-    coefficients = pl.pallas_call(
+    return pl.pallas_call(
         functools.partial(kernel, plan, step_order(pieces, levels)),
-        out_shape=jax.ShapeDtypeStruct((rank, width), half),
-        in_specs=[any_space] * 3,
-        out_specs=pl.BlockSpec(memory_space=pltpu.VMEM),
+        out_shape=jax.ShapeDtypeStruct((leaf, width), half),
+        in_specs=[any_space] * 4,
+        out_specs=any_space,
         scratch_shapes=[
             pltpu.VMEM((pieces, leaf, PIECE), half),
             pltpu.VMEM((leaf, rank), half),
             pltpu.VMEM((rank, leaf), half),
             pltpu.VMEM((levels, rank, 2 * rank), half),
             pltpu.VMEM((levels, pieces, 2 * rank, PIECE), half),
+            pltpu.VMEM((leaf, rank), half),
+            pltpu.VMEM((pieces, leaf, PIECE), half),
             pltpu.SemaphoreType.DMA((pieces,)),
             pltpu.SemaphoreType.DMA,
             pltpu.SemaphoreType.DMA((levels,)),
             pltpu.SemaphoreType.DMA((levels, pieces)),
             pltpu.SemaphoreType.DMA((levels, pieces)),
+            pltpu.SemaphoreType.DMA,
+            pltpu.SemaphoreType.DMA((pieces,)),
         ],
         compiler_params=pltpu.CompilerParams(collective_id=0, has_side_effects=True),
-    )(right_side, projector, translations[0])
-    return jnp.dot(evaluator, coefficients, preferred_element_type=jnp.float32).astype(half)
+    )(right_side, projector, translations[0], evaluator)
 
 
 def solution(mesh):

time: 50.2 us -> 47.6 us (0.948)
  Pallas kernels: 47.2 us -> 45.1 us
  matrix products: 1.53 us -> 0 us
  local copies, waits for them, and re-layouts: 1.32 us -> 2.26 us
    unnamed x2 -> x1, local copies, waits for them, and re-layouts: 0.01 us -> 2.26 us
    pallas_call x1, Pallas kernels: 47.2 us -> 45.1 us  [body(): pl.pallas_call(functools.partial(kernel, plan, step_order(pieces, levels)...]
    dot_general x1 -> x0, matrix products: 1.53 us -> none  [body(): jnp.dot(evaluator, coefficients, preferred_element_type=jnp.float32)]
    convert_element_type x1 -> x0, local copies, waits for them, and re-layouts: 1.32 us -> none  [body(): jnp.dot(evaluator, coefficients, preferred_element_type=jnp.float32)]
where the time goes in v3:
time: 47.6 us; the launch traced here: 47.4 us
  Pallas kernels  45.1 us (95%)
  local copies, waits for them, and re-layouts  2.26 us (5%)
    pallas_call x1, Pallas kernels, body(): pl.pallas_call(functools.partial(kernel, plan, step_order(pieces, levels)...  45.1 us
    unnamed x1, local copies, waits for them, and re-layouts  2.26 us

profile of v3, /device:TPU:0, one launch (start us, length us, event | category | flops | bytes accessed | tf_op | source)
XLA Modules:
  0.0 47.4 jit_solution(3199491662447355279)
XLA Ops:
  0.0 45.1 %shard_map.46 = bf16[512,1024]{1,0:T(8,128)(2,1)} custom-call(bf16[512,1024]{1,0:T(8,128)(2,1)} %right_hbm.1, bf16[512,256]{1,0:T(8,128)(2,1)} %projector_hbm.1, bf16[5,256,512]{2,1,0:T(8,128)(2,1)} %bitcast.1, bf16[512,256]{1,0:T(8,128)(2,1)} %evaluator_hbm.1), custom_call_target="tpu_custom_call" | custom-call | tf_op jit(solution)/shard_map/pallas_call | solution.py:114
  45.2 2.3 %copy.6 = bf16[512,1024]{1,0:T(8,128)(2,1)} copy(bf16[512,1024]{1,0:T(8,128)(2,1)} %shard_map.46) | data formatting | bytes 2097152

commit v4 on v3

--- a/solution.py
+++ b/solution.py
@@ -44,8 +44,6 @@
     evaluator_load = pltpu.make_async_copy(evaluator_hbm, evaluator, evaluator_sem)
     loads[0].start()
     right_loads[0].start()
-    for copy in mapping_loads[:2] + right_loads[1:] + mapping_loads[2:] + [evaluator_load]:
-        copy.start()
 
     partners = []
     for axis, bit in plan:
@@ -70,12 +68,16 @@
         )
 
     loads[0].wait()
+    right_loads[0].wait()
+    for copy in mapping_loads[:2] + right_loads[1:] + mapping_loads[2:] + [evaluator_load]:
+        copy.start()
     projector_t[...] = projector[...].T
     first = True
     mapped = set()
     for p, l in steps:
         if l == 0:
-            right_loads[p].wait()
+            if p > 0:
+                right_loads[p].wait()
             value = jnp.dot(projector_t[...], right[p], preferred_element_type=jnp.float32)
         else:
             if l not in mapped:

time: 47.6 us -> 46.5 us (0.977)
  Pallas kernels: 45.1 us -> 44.1 us
    pallas_call x1, Pallas kernels: 45.1 us -> 44.1 us  [body(): pl.pallas_call(functools.partial(kernel, plan, step_order(pieces, levels)...]
where the time goes in v4:
time: 46.5 us; the launch traced here: 46.3 us
  Pallas kernels  44.1 us (95%)
  local copies, waits for them, and re-layouts  2.26 us (5%)
    pallas_call x1, Pallas kernels, body(): pl.pallas_call(functools.partial(kernel, plan, step_order(pieces, levels)...  44.1 us
    unnamed x1, local copies, waits for them, and re-layouts  2.26 us

profile of v4, /device:TPU:0, one launch (start us, length us, event | category | flops | bytes accessed | tf_op | source)
XLA Modules:
  0.0 46.3 jit_solution(5520126459365973287)
XLA Ops:
  0.0 44.1 %shard_map.46 = bf16[512,1024]{1,0:T(8,128)(2,1)} custom-call(bf16[512,1024]{1,0:T(8,128)(2,1)} %right_hbm.1, bf16[512,256]{1,0:T(8,128)(2,1)} %projector_hbm.1, bf16[5,256,512]{2,1,0:T(8,128)(2,1)} %bitcast.1, bf16[512,256]{1,0:T(8,128)(2,1)} %evaluator_hbm.1), custom_call_target="tpu_custom_call" | custom-call | tf_op jit(solution)/shard_map/pallas_call | solution.py:116
  44.1 2.3 %copy.6 = bf16[512,1024]{1,0:T(8,128)(2,1)} copy(bf16[512,1024]{1,0:T(8,128)(2,1)} %shard_map.46) | data formatting | bytes 2097152

commit v5 on v4

--- a/solution.py
+++ b/solution.py
@@ -71,14 +71,13 @@
     right_loads[0].wait()
     for copy in mapping_loads[:2] + right_loads[1:] + mapping_loads[2:] + [evaluator_load]:
         copy.start()
-    projector_t[...] = projector[...].T
     first = True
     mapped = set()
     for p, l in steps:
         if l == 0:
             if p > 0:
                 right_loads[p].wait()
-            value = jnp.dot(projector_t[...], right[p], preferred_element_type=jnp.float32)
+            value = lax.dot_general(projector[...], right[p], (((0,), (0,)), ((), ())), preferred_element_type=jnp.float32)
         else:
             if l not in mapped:
                 mapping_loads[l - 1].wait()

time: 46.5 us -> 46.6 us (level)
  no operation moved by 1% of the time
where the time goes in v5:
time: 46.6 us; the launch traced here: 46.4 us
  Pallas kernels  44.1 us (95%)
  local copies, waits for them, and re-layouts  2.26 us (5%)
    pallas_call x1, Pallas kernels, body(): pl.pallas_call(functools.partial(kernel, plan, step_order(pieces, levels)...  44.1 us
    unnamed x1, local copies, waits for them, and re-layouts  2.26 us

profile of v5, /device:TPU:0, one launch (start us, length us, event | category | flops | bytes accessed | tf_op | source)
XLA Modules:
  0.0 46.4 jit_solution(10723814011369391349)
XLA Ops:
  0.0 44.1 %shard_map.46 = bf16[512,1024]{1,0:T(8,128)(2,1)} custom-call(bf16[512,1024]{1,0:T(8,128)(2,1)} %right_hbm.1, bf16[512,256]{1,0:T(8,128)(2,1)} %projector_hbm.1, bf16[5,256,512]{2,1,0:T(8,128)(2,1)} %bitcast.1, bf16[512,256]{1,0:T(8,128)(2,1)} %evaluator_hbm.1), custom_call_target="tpu_custom_call" | custom-call | tf_op jit(solution)/shard_map/pallas_call | solution.py:115
  44.1 2.3 %copy.6 = bf16[512,1024]{1,0:T(8,128)(2,1)} copy(bf16[512,1024]{1,0:T(8,128)(2,1)} %shard_map.46) | data formatting | bytes 2097152
